TPU v7x, 32 devices: a whole 2x2x4 slice. The times are simulated.
32 devices in a mesh: wide: 8 (over z, x), narrow: 4 (over y, core).
Axes of the slice: x: 2, y: 2, z: 4, core: 2. Of those that a mesh axis runs over, the one named last changes fastest.
Arguments:
- batch: float32 [128, 768], P('wide'), may hold values from -9 to 9
- targets: float32 [128, 512], P(('wide', 'narrow')), may hold values from -6 to 6
- centers: float32 [4096, 768], P(('wide', 'narrow')), may hold values from -9 to 9
- weights: float32 [4096, 512], P(('wide', 'narrow')), may hold values from -6 to 6
Outputs:
- residual: float32 [128, 512], P(('wide', 'narrow'))
- new_weights: float32 [4096, 512], P(('wide', 'narrow'))
All inputs are finite; a program needn't handle non-finite values.
Results may differ from a plain program's by a relative error of at most 0.0001.
Values sent between devices are 32-bit elements; how exact they have to be, the bound alone decides.
No kernel may reach another device: no remote copies, remote signals or barrier semaphores. Data moves between devices by JAX's collectives and lax.ppermute only.
A program may use at most 64 MiB of HBM per device.

v0:
```python
import functools
import math

import jax
import jax.numpy as jnp
from jax import lax
from jax.experimental import pallas as pl
from jax.experimental.pallas import tpu as pltpu
from jax.sharding import PartitionSpec as P


AXES = ("wide", "narrow")


def odd(number):
    return number.bit_count() % 2


def swap(value, total, masks):
    return lax.ppermute(value, AXES, [(i, i ^ masks[odd(i)]) for i in range(total)])


def flipped(value, place, lead):
    if place is None:
        return value
    shape = (-1, 2, lead << place, value.shape[1])
    return value.reshape(shape)[:, ::-1].reshape(value.shape)


def contract(left, right, dims):
    return lax.dot_general(left, right, (dims, ((), ())), preferred_element_type=jnp.float32)


def parted(value, count):
    parts = []
    for _ in range(count - 1):
        parts.append(value.astype(jnp.bfloat16))
        value = value - parts[-1].astype(jnp.float32)
    return parts + [value.astype(jnp.bfloat16)]


def contract_parts(left, right, dims):
    count, rows = len(left), left[0].shape[0]
    stack = jnp.concatenate(left, axis=0)
    blocks = [contract(stack[: (count - j) * rows], right[j], dims) for j in range(count)]
    total = None
    for place in reversed(range(count)):
        for j in range(place + 1):
            i = place - j
            term = blocks[j][i * rows : (i + 1) * rows]
            total = term if total is None else total + term
    return total


def point_body(centers, *outs):
    spot = centers[...]
    for ref, piece in zip(outs, parted(spot, POINT_PARTS)):
        ref[...] = piece
    outs[-1][...] = jnp.sum(spot * spot, axis=1)[None, :]


def other_body(centers, weights, other_weights, *outs):
    point_body(centers, *outs[: POINT_PARTS + 1])
    gains = parted(weights[...], GAIN_PARTS) + parted(other_weights[...], GAIN_PARTS)
    for ref, piece in zip(outs[POINT_PARTS + 1 :], gains):
        ref[...] = piece


def sum_body(scale, rows, *refs):
    model, rest = refs[: 2 * MODEL], refs[2 * MODEL :]
    value, kernel, other_kernel = rest[-3:]
    both = [jnp.concatenate([a[...], b[...]], axis=0) for a, b in zip(model[: MODEL - 1], model[MODEL:-1])]
    norms = jnp.concatenate([model[MODEL - 1][...], model[-1][...]], axis=1)
    piece = rows[...]
    row_norms = jnp.sum(piece * piece, axis=1, keepdims=True)
    cross = contract_parts(parted(piece, POINT_PARTS), both[:POINT_PARTS], ((1,), (1,)))
    block = jnp.exp(-(row_norms + norms - 2.0 * cross) / piece.shape[1])
    count = kernel.shape[1]
    kernel[...] = block[:, :count]
    other_kernel[...] = block[:, count:]
    value[...] = contract_parts(parted(block, GAIN_PARTS), both[POINT_PARTS:], ((1,), (0,))) * scale
    if len(rest) == 4:
        taken = rest[0]
        lead = taken.shape[0]
        value[:lead] = value[:lead] - taken[...]


def call(body, outs, *operands):
    return pl.pallas_call(
        body,
        out_shape=[jax.ShapeDtypeStruct(shape, dtype) for shape, dtype in outs],
        in_specs=[pl.BlockSpec(memory_space=pltpu.VMEM)] * len(operands),
        out_specs=[pl.BlockSpec(memory_space=pltpu.VMEM)] * len(outs),
        compiler_params=pltpu.CompilerParams(vmem_limit_bytes=LIMIT),
    )(*operands)


LIMIT = 24 * 1024 * 1024
WIDE, NARROW = jnp.float32, jnp.bfloat16


POINT_PARTS, GAIN_PARTS = 3, 2
MODEL = POINT_PARTS + GAIN_PARTS + 1


def point_outs(centers):
    return [(centers.shape, NARROW)] * POINT_PARTS + [((1, centers.shape[0]), WIDE)]


def own_points(centers):
    return call(point_body, point_outs(centers), centers)


def other_parts(centers, weights, other_weights):
    outs = point_outs(centers) + [(weights.shape, NARROW)] * (2 * GAIN_PARTS)
    *others, a, b, c, d = call(other_body, outs, centers, weights, other_weights)
    return others, (a, b), (c, d)


def row_sums(scale, rows, model, *taken):
    count, width = model[POINT_PARTS].shape
    part = rows.shape[0]
    outs = [((part, width), WIDE), ((part, count), WIDE), ((part, count), WIDE)]
    return call(functools.partial(sum_body, scale), outs, rows, *model, *taken)


def turned_body(near, far, swapped, heads, tails):
    kernel = jnp.concatenate([near[...], far[...], swapped[...]], axis=0)
    heads[...], tails[...] = parted(kernel.T, 2)


def turned_parts(near, far, swapped):
    count = near.shape[1]
    shape = (count, near.shape[0] + far.shape[0] + swapped.shape[0])
    return call(turned_body, [(shape, NARROW), (shape, NARROW)], near, far, swapped)


def final_body(rate, heads, tails, weights, *refs):
    values, out, staged, sems = refs[:-3], refs[-3], refs[-2], refs[-1]
    pieces = staged.shape[0]
    size = staged.shape[2]
    copies = []
    for i in range(pieces):
        columns = slice(i * size, (i + 1) * size)
        value = parted(jnp.concatenate([v[:, columns] for v in values], axis=0), 2)
        staged[i] = weights[:, columns] - rate * contract_parts([heads[...], tails[...]], value, ((1,), (0,)))
        copies.append(pltpu.make_async_copy(staged.at[i], out.at[:, columns], sems.at[i]))
        copies[-1].start()
    for copy in copies:
        copy.wait()


def final_update(rate, turned, weights, values):
    count, width = weights.shape
    pieces = max(1, width // PIECE)
    return pl.pallas_call(
        functools.partial(final_body, rate),
        out_shape=jax.ShapeDtypeStruct(weights.shape, jnp.float32),
        in_specs=[pl.BlockSpec(memory_space=pltpu.VMEM)] * (3 + len(values)),
        out_specs=pl.BlockSpec(memory_space=pl.ANY),
        scratch_shapes=[
            pltpu.VMEM((pieces, count, width // pieces), jnp.float32),
            pltpu.SemaphoreType.DMA((pieces,)),
        ],
        compiler_params=pltpu.CompilerParams(vmem_limit_bytes=LIMIT),
    )(*turned, weights, *values)


PIECE = 128


def shards(batch, targets, centers, weights):
    wide = lax.axis_size("wide")
    narrow = lax.axis_size("narrow")
    total = wide * narrow
    own_rows = targets.shape[0]
    own_count = centers.shape[0]
    all_rows = own_rows * total
    pred_scale = 8.0 / math.sqrt(own_count * total)
    spot = lax.axis_index("narrow")
    lane, seat = spot % 2, spot // 2
    seats = narrow // 2
    lead = seats * own_rows
    place = lax.axis_index(AXES)
    parity = sum((place >> b) & 1 for b in range(total.bit_length() - 1)) % 2

    bits = [narrow << b for b in range(wide.bit_length() - 1)]
    first = [bits[0]] + bits[:0:-1]
    second = first[1:] + first[:1]
    spread = list(zip(first, second))
    seat_bits = [2 << b for b in range(seats.bit_length() - 1)]
    line = seat_bits + first[-2::-1]
    other_line = second[:1] + seat_bits + second[1:-1]
    core = (1, 1)

    def across(value, pair):
        return swap(value, total, (pair[0] ^ 1, pair[1] ^ 1))

    def chosen(block, sign):
        pieces = []
        for s in range(seats):
            start = 2 * s * own_rows
            low, high = block[start : start + own_rows], block[start + own_rows : start + 2 * own_rows]
            want = (lane + sign + sum((s ^ seat) >> b & 1 for b in range(seats.bit_length()))) % 2
            pieces.append(jnp.where(want == 0, low, high))
        return jnp.concatenate(pieces, axis=0)

    other_block = across(batch, spread[0])
    other_centers = swap(centers, total, core)
    other_weights = swap(weights, total, core)
    rows = jnp.concatenate([chosen(batch, 0), chosen(other_block, 1)], axis=0)

    mine = (jnp.arange(lead) // own_rows == seat)[:, None]
    taken = jnp.where(mine, jnp.tile(targets, (seats, 1)), 0.0)
    *points, norms = own_points(centers)
    others, gains, other_gains = other_parts(other_centers, weights, other_weights)
    model = [*points, *gains, norms, *others[:-1], *other_gains, others[-1]]
    for pair in spread[1:-2]:
        rows = jnp.concatenate([rows, across(rows, pair)], axis=0)
    near, far = spread[-2:]
    near_rows = across(rows, near)
    far_rows = [across(rows, far)]
    far_rows.append(swap(rows, total, tuple(a ^ b for a, b in zip(near, far))))
    near_rows = jnp.concatenate([rows, near_rows], axis=0)
    early, early_kernel, early_swap = row_sums(pred_scale, near_rows, model, taken)
    far_rows = jnp.concatenate(far_rows, axis=0)
    sent = across(early, spread[-1])
    late, late_kernel, late_swap = row_sums(pred_scale, far_rows, model)
    swapped = swap(jnp.concatenate([early_swap, late_swap], axis=0), total, core)
    value = late + sent

    for pair in zip(line, other_line):
        got = across(value, pair)
        turns = [order.index(m) if m in order else None for m, order in zip(pair, (first, second))]
        here, there = (flipped(got, turn, lead) for turn in turns)
        value = value + (here if turns[0] == turns[1] else jnp.where(parity == 0, here, there))
    near = across(value, spread[-1])
    mate = swap(value, total, core)
    near_mate = swap(near, total, core)
    residual = lax.dynamic_slice_in_dim(near, seat * own_rows, own_rows, axis=0)

    rate = 32.0 / all_rows

    turned = turned_parts(early_kernel, late_kernel, swapped)
    new_weights = final_update(rate, turned, weights, (near, value, near_mate, mate))
    return (residual, new_weights)


def solution(mesh):
    return jax.shard_map(
        shards,
        mesh=mesh,
        in_specs=(
            P("wide", None),
            P(("wide", "narrow"), None),
            P(("wide", "narrow"), None),
            P(("wide", "narrow"), None),
        ),
        out_specs=(P(("wide", "narrow"), None), P(("wide", "narrow"), None)),
        check_vma=False,
    )
```

profile of v0, /device:TPU:0, one launch (start us, length us, event | category | flops | bytes accessed | tf_op | source)
XLA Modules:
  0.0 35.7 jit_solution(3576604735483218764)
XLA Ops:
  0.6 0.0 copy-start.2
  0.6 0.0 copy-start.1
  0.6 2.5 %collective-permute-start = (f32[16,768]{1,0:T(8,128)}, f32[16,768]{1,0:T(8,128)S(1)}, u32[]{:S(2)}, u32[]{:S(2)}) collective-permute-start(f32[16,768]{1,0:T(8,128)} %param.4), channel_id=1, source_target_pairs={{0,5},{1,16},{2,19},{3,6},{4,21},{5,0},{6,3},{7,22},{8,25},{9,12},... | collective-permute-start | bytes 147464 | tf_op jit(solution)/shard_map/ppermute | solution.py:20
  3.1 1.8 %collective-permute-start.3 = (f32[128,768]{1,0:T(8,128)}, f32[128,768]{1,0:T(8,128)S(1)}, u32[]{:S(2)}, u32[]{:S(2)}) collective-permute-start(f32[128,768]{1,0:T(8,128)} %centers.1), channel_id=1, source_target_pairs={{0,1},{1,0},{2,3},{3,2},{4,5},{5,4},{6,7},{7,6},{8,9},{9,8},{10,11... | collective-permute-start | bytes 1179656 | tf_op jit(solution)/shard_map/ppermute | solution.py:20
  4.9 0.0 collective-permute-start.4
  4.9 0.0 copy-done.2
  5.0 0.7 %tile.4 = f32[2,4,512]{2,1,0:T(4,128)S(1)} broadcast(f32[4,512]{1,0:T(4,128)} %param.5), dimensions={1,2} | broadcast | bytes 24576 | tf_op jit(solution)/shard_map/tile | solution.py:214
  5.7 0.0 collective-permute-done
  5.7 2.4 %collective-permute-start.5 = (f32[16,768]{1,0:T(8,128)S(1)}, f32[16,768]{1,0:T(8,128)S(1)}, u32[]{:S(2)}, u32[]{:S(2)}) collective-permute-start(f32[16,768]{1,0:T(8,128)S(1)} %pad_maximum_fusion.1), channel_id=1, source_target_pairs={{0,17},{1,8},{2,11},{3,18},{4,13},{5,20},{6,23},{7,14},{8,1},{9,24... | collective-permute-start | bytes 147464 | tf_op jit(solution)/shard_map/ppermute | solution.py:20
  8.1 1.8 %collective-permute-start.1 = (f32[16,768]{1,0:T(8,128)S(1)}, f32[16,768]{1,0:T(8,128)S(1)}, u32[]{:S(2)}, u32[]{:S(2)}) collective-permute-start(f32[16,768]{1,0:T(8,128)S(1)} %pad_maximum_fusion.1), channel_id=1, source_target_pairs={{0,9},{1,4},{2,7},{3,10},{4,1},{5,12},{6,15},{7,2},{8,13},{9,0},{1... | collective-permute-start | bytes 147464 | tf_op jit(solution)/shard_map/ppermute | solution.py:20
  9.9 0.0 collective-permute-start.2
  9.9 0.1 broadcast_select_fusion.refs_12_
  10.0 0.0 copy-done.1
  10.0 0.0 copy-start
  10.0 0.2 shard_map.59
  10.2 0.0 collective-permute-done.5
  10.2 0.1 concatenate.15.rows
  10.3 0.0 collective-permute-done.4.other_weights
  10.3 0.0 collective-permute-done.3.centers
  10.3 0.7 %copy-done = f32[128,512]{1,0:T(8,128)S(1)} copy-done((f32[128,512]{1,0:T(8,128)S(1)}, f32[128,512]{1,0:T(8,128)}, u32[]{:S(2)}) %copy-start) | copy-done | bytes 262168
  10.9 0.2 shard_map.60
  11.2 0.8 %shard_map.62 = (f32[32,512]{1,0:T(8,128)S(1)}, f32[32,128]{1,0:T(8,128)S(1)}, f32[32,128]{1,0:T(8,128)S(1)}) custom-call(f32[32,768]{1,0:T(8,128)S(1)} %concatenate.15.rows, bf16[128,768]{1,0:T(8,128)(2,1)S(1)} %get-tuple-element.22.refs_0_, bf16[128,768]{1,0:T(8,128)(2,1)S(1)} %get-tuple-element.23.refs_1_, ...), custom_call_target="tpu_custom_call" | custom-call | tf_op jit(solution)/shard_map/pallas_call | solution.py:89
  12.0 0.9 %collective-permute-start.6 = (f32[32,512]{1,0:T(8,128)S(1)}, f32[32,512]{1,0:T(8,128)S(1)}, u32[]{:S(2)}, u32[]{:S(2)}) collective-permute-start(f32[32,512]{1,0:T(8,128)S(1)} %get-tuple-element.35), channel_id=1, source_target_pairs={{0,9},{1,4},{2,7},{3,10},{4,1},{5,12},{6,15},{7,2},{8,13},{9,0},{1... | collective-permute-start | bytes 196616 | tf_op jit(solution)/shard_map/ppermute | solution.py:20
  12.9 0.0 collective-permute-done.1
  12.9 3.0 %collective-permute-done.2 = f32[16,768]{1,0:T(8,128)S(1)} collective-permute-done((f32[16,768]{1,0:T(8,128)S(1)}, f32[16,768]{1,0:T(8,128)S(1)}, u32[]{:S(2)}, u32[]{:S(2)}) %collective-permute-start.2) | collective-permute-done | bytes 49184 | tf_op jit(solution)/shard_map/ppermute | solution.py:20
  15.9 0.8 %shard_map.61 = (f32[32,512]{1,0:T(8,128)S(1)}, f32[32,128]{1,0:T(8,128)S(1)}, f32[32,128]{1,0:T(8,128)S(1)}) custom-call(f32[32,768]{1,0:T(8,128)S(1)} %pad_maximum_fusion.rows, bf16[128,768]{1,0:T(8,128)(2,1)S(1)} %get-tuple-element.22.refs_0_, bf16[128,768]{1,0:T(8,128)(2,1)S(1)} %get-tuple-element.23.refs_1_, ...), custom_call_target="tpu_custom_call" | custom-call | tf_op jit(solution)/shard_map/pallas_call | solution.py:89
  16.7 0.0 collective-permute-done.6
  16.7 0.5 %collective-permute-start.7 = (f32[32,512]{1,0:T(8,128)S(1)}, f32[32,512]{1,0:T(8,128)S(1)}, u32[]{:S(2)}, u32[]{:S(2)}) collective-permute-start(f32[32,512]{1,0:T(8,128)S(1)} %add.91), channel_id=1, source_target_pairs={{0,3},{1,16},{2,19},{3,0},{4,21},{5,6},{6,5},{7,22},{8,25},{9,10},... | collective-permute-start | bytes 196616 | tf_op jit(solution)/shard_map/ppermute | solution.py:20
  17.3 3.2 %collective-permute-done.7 = f32[32,512]{1,0:T(8,128)S(1)} collective-permute-done((f32[32,512]{1,0:T(8,128)S(1)}, f32[32,512]{1,0:T(8,128)S(1)}, u32[]{:S(2)}, u32[]{:S(2)}) %collective-permute-start.7) | collective-permute-done | bytes 65568 | tf_op jit(solution)/shard_map/ppermute | solution.py:20
  20.5 1.9 %collective-permute-start.8 = (f32[32,512]{1,0:T(8,128)S(1)}, f32[32,512]{1,0:T(8,128)S(1)}, u32[]{:S(2)}, u32[]{:S(2)}) collective-permute-start(f32[32,512]{1,0:T(8,128)S(1)} %fusion.2), channel_id=1, source_target_pairs={{0,17},{1,2},{2,1},{3,18},{4,7},{5,20},{6,23},{7,4},{8,11},{9,24},... | collective-permute-start | bytes 196616 | tf_op jit(solution)/shard_map/ppermute | solution.py:20
  22.4 3.4 %collective-permute-done.8 = f32[32,512]{1,0:T(8,128)S(1)} collective-permute-done((f32[32,512]{1,0:T(8,128)S(1)}, f32[32,512]{1,0:T(8,128)S(1)}, u32[]{:S(2)}, u32[]{:S(2)}) %collective-permute-start.8) | collective-permute-done | bytes 65568 | tf_op jit(solution)/shard_map/ppermute | solution.py:20
  25.9 0.8 %collective-permute-start.9 = (f32[32,512]{1,0:T(8,128)S(1)}, f32[32,512]{1,0:T(8,128)S(1)}, u32[]{:S(2)}, u32[]{:S(2)}) collective-permute-start(f32[32,512]{1,0:T(8,128)S(1)} %fusion.1), channel_id=1, source_target_pairs={{0,5},{1,8},{2,11},{3,6},{4,13},{5,0},{6,3},{7,14},{8,1},{9,12},{1... | collective-permute-start | bytes 196616 | tf_op jit(solution)/shard_map/ppermute | solution.py:20
  26.7 3.0 %collective-permute-done.9 = f32[32,512]{1,0:T(8,128)S(1)} collective-permute-done((f32[32,512]{1,0:T(8,128)S(1)}, f32[32,512]{1,0:T(8,128)S(1)}, u32[]{:S(2)}, u32[]{:S(2)}) %collective-permute-start.9) | collective-permute-done | bytes 65568 | tf_op jit(solution)/shard_map/ppermute | solution.py:20
  29.7 0.1 collective-permute-start.10
  29.8 0.1 collective-permute-start.11
  29.9 1.2 %collective-permute-done.11.swapped = f32[64,128]{1,0:T(8,128)S(1)} collective-permute-done((f32[64,128]{1,0:T(8,128)S(1)}, f32[64,128]{1,0:T(8,128)S(1)}, u32[]{:S(2)}, u32[]{:S(2)}) %collective-permute-start.11) | collective-permute-done | bytes 32800 | tf_op jit(solution)/shard_map/ppermute | solution.py:20
  31.1 0.1 shard_map.63
  31.2 0.2 collective-permute-start.13
  31.4 2.1 %collective-permute-done.10.refs_0_ = f32[32,512]{1,0:T(8,128)S(1)} collective-permute-done((f32[32,512]{1,0:T(8,128)S(1)}, f32[32,512]{1,0:T(8,128)S(1)}, u32[]{:S(2)}, u32[]{:S(2)}) %collective-permute-start.10) | collective-permute-done | bytes 65568 | tf_op jit(solution)/shard_map/ppermute | solution.py:20
  33.5 0.0 collective-permute-start.12
  33.5 0.6 %constant_dynamic-slice_fusion = f32[4,512]{1,0:T(4,128)} fusion(f32[32,512]{1,0:T(8,128)S(1)} %collective-permute-done.10.refs_0_, s32[]{:T(128)S(6)} %select_n.110), kind=kLoop, calls=%fused_computation.19 | loop fusion | bytes 16388 | tf_op jit(solution)/shard_map/dynamic_slice | solution.py:240
  34.1 0.0 collective-permute-done.13.refs_3_
  34.1 0.6 %collective-permute-done.12.refs_2_ = f32[32,512]{1,0:T(8,128)S(1)} collective-permute-done((f32[32,512]{1,0:T(8,128)S(1)}, f32[32,512]{1,0:T(8,128)S(1)}, u32[]{:S(2)}, u32[]{:S(2)}) %collective-permute-start.12) | collective-permute-done | bytes 65568 | tf_op jit(solution)/shard_map/ppermute | solution.py:20
  34.7 0.9 %shard_map.64 = f32[128,512]{1,0:T(8,128)} custom-call(bf16[128,128]{1,0:T(8,128)(2,1)S(1)} %get-tuple-element.40.heads, bf16[128,128]{1,0:T(8,128)(2,1)S(1)} %get-tuple-element.41.tails, f32[128,512]{1,0:T(8,128)S(1)} %copy-done, f32[32,512]{1,0:T(8,128)S(1)} %collective-permute-done.10.refs_0_, f32[32,512]{1,0:T(8,128)S(1)} %fusion.refs_1_, ...), custom_call_target="tpu_custom_call" | custom-call | tf_op jit(solution)/shard_map/pallas_call | solution.py:156
  (15 shorter events, 0.1 us)
Async XLA Ops:
  0.6 4.3 %copy-start.2 = (f32[16,768]{1,0:T(8,128)S(1)}, f32[16,768]{1,0:T(8,128)}, u32[]{:S(2)}) copy-start(f32[16,768]{1,0:T(8,128)} %param.4) | copy-start | bytes 147460
  0.6 9.3 %copy-start.1 = (f32[128,768]{1,0:T(8,128)S(1)}, f32[128,768]{1,0:T(8,128)}, u32[]{:S(2)}) copy-start(f32[128,768]{1,0:T(8,128)} %centers.1) | copy-start | bytes 1179652
  0.6 5.0 %collective-permute-start = (f32[16,768]{1,0:T(8,128)}, f32[16,768]{1,0:T(8,128)S(1)}, u32[]{:S(2)}, u32[]{:S(2)}) collective-permute-start(f32[16,768]{1,0:T(8,128)} %param.4), channel_id=1, source_target_pairs={{0,5},{1,16},{2,19},{3,6},{4,21},{5,0},{6,3},{7,22},{8,25},{9,12},... | collective-permute-start | bytes 147464 | tf_op jit(solution)/shard_map/ppermute | solution.py:20
  3.1 7.1 %collective-permute-start.3 = (f32[128,768]{1,0:T(8,128)}, f32[128,768]{1,0:T(8,128)S(1)}, u32[]{:S(2)}, u32[]{:S(2)}) collective-permute-start(f32[128,768]{1,0:T(8,128)} %centers.1), channel_id=1, source_target_pairs={{0,1},{1,0},{2,3},{3,2},{4,5},{5,4},{6,7},{7,6},{8,9},{9,8},{10,11... | collective-permute-start | bytes 1179656 | tf_op jit(solution)/shard_map/ppermute | solution.py:20
  4.9 5.4 %collective-permute-start.4 = (f32[128,512]{1,0:T(8,128)}, f32[128,512]{1,0:T(8,128)S(1)}, u32[]{:S(2)}, u32[]{:S(2)}) collective-permute-start(f32[128,512]{1,0:T(8,128)} %weights.3), channel_id=1, source_target_pairs={{0,1},{1,0},{2,3},{3,2},{4,5},{5,4},{6,7},{7,6},{8,9},{9,8},{10,11... | collective-permute-start | bytes 786440 | tf_op jit(solution)/shard_map/ppermute | solution.py:20
  5.7 4.5 %collective-permute-start.5 = (f32[16,768]{1,0:T(8,128)S(1)}, f32[16,768]{1,0:T(8,128)S(1)}, u32[]{:S(2)}, u32[]{:S(2)}) collective-permute-start(f32[16,768]{1,0:T(8,128)S(1)} %pad_maximum_fusion.1), channel_id=1, source_target_pairs={{0,17},{1,8},{2,11},{3,18},{4,13},{5,20},{6,23},{7,14},{8,1},{9,24... | collective-permute-start | bytes 147464 | tf_op jit(solution)/shard_map/ppermute | solution.py:20
  8.1 4.8 %collective-permute-start.1 = (f32[16,768]{1,0:T(8,128)S(1)}, f32[16,768]{1,0:T(8,128)S(1)}, u32[]{:S(2)}, u32[]{:S(2)}) collective-permute-start(f32[16,768]{1,0:T(8,128)S(1)} %pad_maximum_fusion.1), channel_id=1, source_target_pairs={{0,9},{1,4},{2,7},{3,10},{4,1},{5,12},{6,15},{7,2},{8,13},{9,0},{1... | collective-permute-start | bytes 147464 | tf_op jit(solution)/shard_map/ppermute | solution.py:20
  9.9 6.0 %collective-permute-start.2 = (f32[16,768]{1,0:T(8,128)S(1)}, f32[16,768]{1,0:T(8,128)S(1)}, u32[]{:S(2)}, u32[]{:S(2)}) collective-permute-start(f32[16,768]{1,0:T(8,128)S(1)} %pad_maximum_fusion.1), channel_id=1, source_target_pairs={{0,24},{1,13},{2,14},{3,27},{4,8},{5,29},{6,30},{7,11},{8,4},{9,17... | collective-permute-start | bytes 147464 | tf_op jit(solution)/shard_map/ppermute | solution.py:20
  10.0 1.0 %copy-start = (f32[128,512]{1,0:T(8,128)S(1)}, f32[128,512]{1,0:T(8,128)}, u32[]{:S(2)}) copy-start(f32[128,512]{1,0:T(8,128)} %weights.3) | copy-start | bytes 786436
  12.0 4.7 %collective-permute-start.6 = (f32[32,512]{1,0:T(8,128)S(1)}, f32[32,512]{1,0:T(8,128)S(1)}, u32[]{:S(2)}, u32[]{:S(2)}) collective-permute-start(f32[32,512]{1,0:T(8,128)S(1)} %get-tuple-element.35), channel_id=1, source_target_pairs={{0,9},{1,4},{2,7},{3,10},{4,1},{5,12},{6,15},{7,2},{8,13},{9,0},{1... | collective-permute-start | bytes 196616 | tf_op jit(solution)/shard_map/ppermute | solution.py:20
  16.7 3.8 %collective-permute-start.7 = (f32[32,512]{1,0:T(8,128)S(1)}, f32[32,512]{1,0:T(8,128)S(1)}, u32[]{:S(2)}, u32[]{:S(2)}) collective-permute-start(f32[32,512]{1,0:T(8,128)S(1)} %add.91), channel_id=1, source_target_pairs={{0,3},{1,16},{2,19},{3,0},{4,21},{5,6},{6,5},{7,22},{8,25},{9,10},... | collective-permute-start | bytes 196616 | tf_op jit(solution)/shard_map/ppermute | solution.py:20
  20.5 5.4 %collective-permute-start.8 = (f32[32,512]{1,0:T(8,128)S(1)}, f32[32,512]{1,0:T(8,128)S(1)}, u32[]{:S(2)}, u32[]{:S(2)}) collective-permute-start(f32[32,512]{1,0:T(8,128)S(1)} %fusion.2), channel_id=1, source_target_pairs={{0,17},{1,2},{2,1},{3,18},{4,7},{5,20},{6,23},{7,4},{8,11},{9,24},... | collective-permute-start | bytes 196616 | tf_op jit(solution)/shard_map/ppermute | solution.py:20
  25.9 3.8 %collective-permute-start.9 = (f32[32,512]{1,0:T(8,128)S(1)}, f32[32,512]{1,0:T(8,128)S(1)}, u32[]{:S(2)}, u32[]{:S(2)}) collective-permute-start(f32[32,512]{1,0:T(8,128)S(1)} %fusion.1), channel_id=1, source_target_pairs={{0,5},{1,8},{2,11},{3,6},{4,13},{5,0},{6,3},{7,14},{8,1},{9,12},{1... | collective-permute-start | bytes 196616 | tf_op jit(solution)/shard_map/ppermute | solution.py:20
  29.7 3.8 %collective-permute-start.10 = (f32[32,512]{1,0:T(8,128)S(1)}, f32[32,512]{1,0:T(8,128)S(1)}, u32[]{:S(2)}, u32[]{:S(2)}) collective-permute-start(f32[32,512]{1,0:T(8,128)S(1)} %fusion.refs_1_), channel_id=1, source_target_pairs={{0,9},{1,4},{2,7},{3,10},{4,1},{5,12},{6,15},{7,2},{8,13},{9,0},{1... | collective-permute-start | bytes 196616 | tf_op jit(solution)/shard_map/ppermute | solution.py:20
  29.8 1.3 %collective-permute-start.11 = (f32[64,128]{1,0:T(8,128)S(1)}, f32[64,128]{1,0:T(8,128)S(1)}, u32[]{:S(2)}, u32[]{:S(2)}) collective-permute-start(f32[64,128]{1,0:T(8,128)S(1)} %pad_maximum_fusion.2), channel_id=1, source_target_pairs={{0,1},{1,0},{2,3},{3,2},{4,5},{5,4},{6,7},{7,6},{8,9},{9,8},{10,11... | collective-permute-start | bytes 98312 | tf_op jit(solution)/shard_map/ppermute | solution.py:20
  31.2 2.9 %collective-permute-start.13 = (f32[32,512]{1,0:T(8,128)S(1)}, f32[32,512]{1,0:T(8,128)S(1)}, u32[]{:S(2)}, u32[]{:S(2)}) collective-permute-start(f32[32,512]{1,0:T(8,128)S(1)} %fusion.refs_1_), channel_id=1, source_target_pairs={{0,1},{1,0},{2,3},{3,2},{4,5},{5,4},{6,7},{7,6},{8,9},{9,8},{10,11... | collective-permute-start | bytes 196616 | tf_op jit(solution)/shard_map/ppermute | solution.py:20
  33.5 1.3 %collective-permute-start.12 = (f32[32,512]{1,0:T(8,128)S(1)}, f32[32,512]{1,0:T(8,128)S(1)}, u32[]{:S(2)}, u32[]{:S(2)}) collective-permute-start(f32[32,512]{1,0:T(8,128)S(1)} %collective-permute-done.10.refs_0_), channel_id=1, source_target_pairs={{0,1},{1,0},{2,3},{3,2},{4,5},{5,4},{6,7},{7,6},{8,9},{9,8},{10,11... | collective-permute-start | bytes 196616 | tf_op jit(solution)/shard_map/ppermute | solution.py:20
where the time goes:
time: 35.9 us; the launch traced here: 35.7 us
  waiting for transfers between devices  16.6 us (46%)
  starting transfers between devices  12.9 us (36%)
  Pallas kernels  3.06 us (9%)
  local copies, waits for them, and re-layouts  2.06 us (6%)
  between operations  0.8 us (2%)
    ppermute x14, waiting for transfers between devices, swap(): lax.ppermute(value, AXES, [(i, i ^ masks[odd(i)]) for i in range(total)])  16.6 us
    ppermute x14, starting transfers between devices, swap(): lax.ppermute(value, AXES, [(i, i ^ masks[odd(i)]) for i in range(total)])  12.9 us
    pallas_call x5, Pallas kernels, call(): pl.pallas_call(body, out_shape=[jax.ShapeDtypeStruct(shape, dtype) for sh...  2.12 us
    pallas_call x1, Pallas kernels, final_update(): pl.pallas_call(functools.partial(final_body, rate), out_shape=jax.ShapeDt...  0.94 us
  transfers between devices with their start and end apart: 14, of which 7 were waited for; matrix products, arithmetic and copies ran while one was open for 4% of the time, Pallas kernels for 6%

commit v1 on v0

--- a/solution.py
+++ b/solution.py
@@ -227,22 +227,30 @@
     sent = across(early, spread[-1])
     late, late_kernel, late_swap = row_sums(pred_scale, far_rows, model)
     swapped = swap(jnp.concatenate([early_swap, late_swap], axis=0), total, core)
+    turned = turned_parts(early_kernel, late_kernel, swapped)
     value = late + sent
 
-    for pair in zip(line, other_line):
-        got = across(value, pair)
+    def turned_rows(got, pair):
         turns = [order.index(m) if m in order else None for m, order in zip(pair, (first, second))]
         here, there = (flipped(got, turn, lead) for turn in turns)
-        value = value + (here if turns[0] == turns[1] else jnp.where(parity == 0, here, there))
-    near = across(value, spread[-1])
-    mate = swap(value, total, core)
-    near_mate = swap(near, total, core)
-    residual = lax.dynamic_slice_in_dim(near, seat * own_rows, own_rows, axis=0)
+        return here if turns[0] == turns[1] else jnp.where(parity == 0, here, there)
+
+    *inner, last = zip(line, other_line)
+    for pair in inner:
+        got = across(value, pair)
+        value = value + turned_rows(got, pair)
+    side = across(value, last)
+    corner = swap(value, total, tuple(a ^ b for a, b in zip(last, far)))
+    near_sum = across(value, far)
+    value = value + turned_rows(side, last)
+    near_sum = near_sum + turned_rows(corner, last)
+    full = jnp.concatenate([near_sum, value], axis=0)
+    partner = swap(full, total, core)
+    residual = lax.dynamic_slice_in_dim(near_sum, seat * own_rows, own_rows, axis=0)
 
     rate = 32.0 / all_rows
 
-    turned = turned_parts(early_kernel, late_kernel, swapped)
-    new_weights = final_update(rate, turned, weights, (near, value, near_mate, mate))
+    new_weights = final_update(rate, turned, weights, (full, partner))
     return (residual, new_weights)
 
 

time: 35.9 us -> 34.8 us (0.969)
  waiting for transfers between devices: 16.6 us -> 13.2 us
  starting transfers between devices: 12.9 us -> 15.2 us
    ppermute x14, waiting for transfers between devices: 16.6 us -> 13.2 us  [swap(): lax.ppermute(value, AXES, [(i, i ^ masks[odd(i)]) for i in range(total)])]
    ppermute x14, starting transfers between devices: 12.9 us -> 15.2 us  [swap(): lax.ppermute(value, AXES, [(i, i ^ masks[odd(i)]) for i in range(total)])]
  transfers between devices with their start and end apart: 14 -> 14, of which waited for: 7 -> 6; matrix products, arithmetic and copies ran while one was open for 4% -> 5% of each run, Pallas kernels for 6% -> 6%
where the time goes in v1:
time: 34.8 us; the launch traced here: 34.6 us
  starting transfers between devices  15.2 us (44%)
  waiting for transfers between devices  13.2 us (38%)
  Pallas kernels  3.07 us (9%)
  local copies, waits for them, and re-layouts  2.08 us (6%)
  between operations  0.81 us (2%)
    ppermute x14, starting transfers between devices, swap(): lax.ppermute(value, AXES, [(i, i ^ masks[odd(i)]) for i in range(total)])  15.2 us
    ppermute x14, waiting for transfers between devices, swap(): lax.ppermute(value, AXES, [(i, i ^ masks[odd(i)]) for i in range(total)])  13.2 us
    pallas_call x5, Pallas kernels, call(): pl.pallas_call(body, out_shape=[jax.ShapeDtypeStruct(shape, dtype) for sh...  2.12 us
    pallas_call x1, Pallas kernels, final_update(): pl.pallas_call(functools.partial(final_body, rate), out_shape=jax.ShapeDt...  0.95 us
    another operation x2, local copies, waits for them, and re-layouts, shards(): taken = jnp.where(mine, jnp.tile(targets, (seats, 1)), 0.0)  0.71 us
  transfers between devices with their start and end apart: 14, of which 6 were waited for; matrix products, arithmetic and copies ran while one was open for 5% of the time, Pallas kernels for 6%

profile of v1, /device:TPU:0, one launch (start us, length us, event | category | flops | bytes accessed | tf_op | source)
XLA Modules:
  0.0 34.6 jit_solution(9466911353766596828)
XLA Ops:
  0.6 0.0 copy-start.2
  0.6 0.0 copy-start.1
  0.6 2.5 %collective-permute-start = (f32[16,768]{1,0:T(8,128)}, f32[16,768]{1,0:T(8,128)S(1)}, u32[]{:S(2)}, u32[]{:S(2)}) collective-permute-start(f32[16,768]{1,0:T(8,128)} %param.4), channel_id=1, source_target_pairs={{0,5},{1,16},{2,19},{3,6},{4,21},{5,0},{6,3},{7,22},{8,25},{9,12},... | collective-permute-start | bytes 147464 | tf_op jit(solution)/shard_map/ppermute | solution.py:20
  3.1 1.8 %collective-permute-start.3 = (f32[128,768]{1,0:T(8,128)}, f32[128,768]{1,0:T(8,128)S(1)}, u32[]{:S(2)}, u32[]{:S(2)}) collective-permute-start(f32[128,768]{1,0:T(8,128)} %centers.1), channel_id=1, source_target_pairs={{0,1},{1,0},{2,3},{3,2},{4,5},{5,4},{6,7},{7,6},{8,9},{9,8},{10,11... | collective-permute-start | bytes 1179656 | tf_op jit(solution)/shard_map/ppermute | solution.py:20
  4.9 0.0 collective-permute-start.4
  4.9 0.0 copy-done.2
  5.0 0.7 %tile.4 = f32[2,4,512]{2,1,0:T(4,128)S(1)} broadcast(f32[4,512]{1,0:T(4,128)} %param.5), dimensions={1,2} | broadcast | bytes 24576 | tf_op jit(solution)/shard_map/tile | solution.py:214
  5.7 0.0 collective-permute-done
  5.7 2.4 %collective-permute-start.5 = (f32[16,768]{1,0:T(8,128)S(1)}, f32[16,768]{1,0:T(8,128)S(1)}, u32[]{:S(2)}, u32[]{:S(2)}) collective-permute-start(f32[16,768]{1,0:T(8,128)S(1)} %pad_maximum_fusion.2), channel_id=1, source_target_pairs={{0,17},{1,8},{2,11},{3,18},{4,13},{5,20},{6,23},{7,14},{8,1},{9,24... | collective-permute-start | bytes 147464 | tf_op jit(solution)/shard_map/ppermute | solution.py:20
  8.1 1.8 %collective-permute-start.1 = (f32[16,768]{1,0:T(8,128)S(1)}, f32[16,768]{1,0:T(8,128)S(1)}, u32[]{:S(2)}, u32[]{:S(2)}) collective-permute-start(f32[16,768]{1,0:T(8,128)S(1)} %pad_maximum_fusion.2), channel_id=1, source_target_pairs={{0,9},{1,4},{2,7},{3,10},{4,1},{5,12},{6,15},{7,2},{8,13},{9,0},{1... | collective-permute-start | bytes 147464 | tf_op jit(solution)/shard_map/ppermute | solution.py:20
  9.9 0.0 collective-permute-start.2
  9.9 0.1 broadcast_select_fusion.refs_12_
  10.0 0.0 copy-done.1
  10.0 0.0 copy-start
  10.0 0.2 shard_map.59
  10.2 0.0 collective-permute-done.5
  10.2 0.1 concatenate.18.rows
  10.3 0.0 collective-permute-done.4.other_weights
  10.3 0.0 collective-permute-done.3.centers
  10.3 0.7 %copy-done = f32[128,512]{1,0:T(8,128)S(1)} copy-done((f32[128,512]{1,0:T(8,128)S(1)}, f32[128,512]{1,0:T(8,128)}, u32[]{:S(2)}) %copy-start) | copy-done | bytes 262168
  10.9 0.2 shard_map.60
  11.2 0.8 %shard_map.62 = (f32[32,512]{1,0:T(8,128)S(1)}, f32[32,128]{1,0:T(8,128)S(1)}, f32[32,128]{1,0:T(8,128)S(1)}) custom-call(f32[32,768]{1,0:T(8,128)S(1)} %concatenate.18.rows, bf16[128,768]{1,0:T(8,128)(2,1)S(1)} %get-tuple-element.22.refs_0_, bf16[128,768]{1,0:T(8,128)(2,1)S(1)} %get-tuple-element.23.refs_1_, ...), custom_call_target="tpu_custom_call" | custom-call | tf_op jit(solution)/shard_map/pallas_call | solution.py:89
  12.0 0.9 %collective-permute-start.6 = (f32[32,512]{1,0:T(8,128)S(1)}, f32[32,512]{1,0:T(8,128)S(1)}, u32[]{:S(2)}, u32[]{:S(2)}) collective-permute-start(f32[32,512]{1,0:T(8,128)S(1)} %get-tuple-element.35), channel_id=1, source_target_pairs={{0,9},{1,4},{2,7},{3,10},{4,1},{5,12},{6,15},{7,2},{8,13},{9,0},{1... | collective-permute-start | bytes 196616 | tf_op jit(solution)/shard_map/ppermute | solution.py:20
  12.9 0.0 collective-permute-done.1
  12.9 3.0 %collective-permute-done.2 = f32[16,768]{1,0:T(8,128)S(1)} collective-permute-done((f32[16,768]{1,0:T(8,128)S(1)}, f32[16,768]{1,0:T(8,128)S(1)}, u32[]{:S(2)}, u32[]{:S(2)}) %collective-permute-start.2) | collective-permute-done | bytes 49184 | tf_op jit(solution)/shard_map/ppermute | solution.py:20
  15.9 0.8 %shard_map.61 = (f32[32,512]{1,0:T(8,128)S(1)}, f32[32,128]{1,0:T(8,128)S(1)}, f32[32,128]{1,0:T(8,128)S(1)}) custom-call(f32[32,768]{1,0:T(8,128)S(1)} %pad_maximum_fusion.1.rows, bf16[128,768]{1,0:T(8,128)(2,1)S(1)} %get-tuple-element.22.refs_0_, bf16[128,768]{1,0:T(8,128)(2,1)S(1)} %get-tuple-element.23.refs_1_, ...), custom_call_target="tpu_custom_call" | custom-call | tf_op jit(solution)/shard_map/pallas_call | solution.py:89
  16.7 0.0 collective-permute-done.6
  16.7 0.5 %collective-permute-start.7 = (f32[32,512]{1,0:T(8,128)S(1)}, f32[32,512]{1,0:T(8,128)S(1)}, u32[]{:S(2)}, u32[]{:S(2)}) collective-permute-start(f32[32,512]{1,0:T(8,128)S(1)} %add.94), channel_id=1, source_target_pairs={{0,3},{1,16},{2,19},{3,0},{4,21},{5,6},{6,5},{7,22},{8,25},{9,10},... | collective-permute-start | bytes 196616 | tf_op jit(solution)/shard_map/ppermute | solution.py:20
  17.3 3.2 %collective-permute-done.7 = f32[32,512]{1,0:T(8,128)S(1)} collective-permute-done((f32[32,512]{1,0:T(8,128)S(1)}, f32[32,512]{1,0:T(8,128)S(1)}, u32[]{:S(2)}, u32[]{:S(2)}) %collective-permute-start.7) | collective-permute-done | bytes 65568 | tf_op jit(solution)/shard_map/ppermute | solution.py:20
  20.5 1.9 %collective-permute-start.8 = (f32[32,512]{1,0:T(8,128)S(1)}, f32[32,512]{1,0:T(8,128)S(1)}, u32[]{:S(2)}, u32[]{:S(2)}) collective-permute-start(f32[32,512]{1,0:T(8,128)S(1)} %fusion.3), channel_id=1, source_target_pairs={{0,17},{1,2},{2,1},{3,18},{4,7},{5,20},{6,23},{7,4},{8,11},{9,24},... | collective-permute-start | bytes 196616 | tf_op jit(solution)/shard_map/ppermute | solution.py:20
  22.4 3.4 %collective-permute-done.8 = f32[32,512]{1,0:T(8,128)S(1)} collective-permute-done((f32[32,512]{1,0:T(8,128)S(1)}, f32[32,512]{1,0:T(8,128)S(1)}, u32[]{:S(2)}, u32[]{:S(2)}) %collective-permute-start.8) | collective-permute-done | bytes 65568 | tf_op jit(solution)/shard_map/ppermute | solution.py:20
  25.9 0.8 %collective-permute-start.12 = (f32[32,512]{1,0:T(8,128)S(1)}, f32[32,512]{1,0:T(8,128)S(1)}, u32[]{:S(2)}, u32[]{:S(2)}) collective-permute-start(f32[32,512]{1,0:T(8,128)S(1)} %fusion.2), channel_id=1, source_target_pairs={{0,5},{1,8},{2,11},{3,6},{4,13},{5,0},{6,3},{7,14},{8,1},{9,12},{1... | collective-permute-start | bytes 196616 | tf_op jit(solution)/shard_map/ppermute | solution.py:20
  26.7 0.0 collective-permute-start.11
  26.7 0.9 %collective-permute-start.10 = (f32[32,512]{1,0:T(8,128)S(1)}, f32[32,512]{1,0:T(8,128)S(1)}, u32[]{:S(2)}, u32[]{:S(2)}) collective-permute-start(f32[32,512]{1,0:T(8,128)S(1)} %fusion.2), channel_id=1, source_target_pairs={{0,12},{1,13},{2,14},{3,15},{4,8},{5,9},{6,10},{7,11},{8,4},{9,5},... | collective-permute-start | bytes 196616 | tf_op jit(solution)/shard_map/ppermute | solution.py:20
  27.6 1.4 %collective-permute-start.9 = (f32[32,512]{1,0:T(8,128)S(1)}, f32[32,512]{1,0:T(8,128)S(1)}, u32[]{:S(2)}, u32[]{:S(2)}) collective-permute-start(f32[32,512]{1,0:T(8,128)S(1)} %fusion.2), channel_id=1, source_target_pairs={{0,9},{1,4},{2,7},{3,10},{4,1},{5,12},{6,15},{7,2},{8,13},{9,0},{1... | collective-permute-start | bytes 196616 | tf_op jit(solution)/shard_map/ppermute | solution.py:20
  28.9 0.7 %collective-permute-done.12 = f32[32,512]{1,0:T(8,128)S(1)} collective-permute-done((f32[32,512]{1,0:T(8,128)S(1)}, f32[32,512]{1,0:T(8,128)S(1)}, u32[]{:S(2)}, u32[]{:S(2)}) %collective-permute-start.12) | collective-permute-done | bytes 65568 | tf_op jit(solution)/shard_map/ppermute | solution.py:20
  29.7 2.5 %collective-permute-done.10 = f32[32,512]{1,0:T(8,128)S(1)} collective-permute-done((f32[32,512]{1,0:T(8,128)S(1)}, f32[32,512]{1,0:T(8,128)S(1)}, u32[]{:S(2)}, u32[]{:S(2)}) %collective-permute-start.10) | collective-permute-done | bytes 65568 | tf_op jit(solution)/shard_map/ppermute | solution.py:20
  32.2 0.0 collective-permute-done.9
  32.2 0.5 %collective-permute-start.13 = (f32[64,512]{1,0:T(8,128)S(1)}, f32[64,512]{1,0:T(8,128)S(1)}, u32[]{:S(2)}, u32[]{:S(2)}) collective-permute-start(f32[64,512]{1,0:T(8,128)S(1)} %pad_maximum_fusion.refs_0_), channel_id=1, source_target_pairs={{0,1},{1,0},{2,3},{3,2},{4,5},{5,4},{6,7},{7,6},{8,9},{9,8},{10,11... | collective-permute-start | bytes 393224 | tf_op jit(solution)/shard_map/ppermute | solution.py:20
  32.7 0.0 collective-permute-done.11.swapped
  32.7 0.1 shard_map.63
  32.8 0.6 %constant_dynamic-slice_fusion = f32[4,512]{1,0:T(4,128)} fusion(f32[32,512]{1,0:T(8,128)S(1)} %fusion.1, s32[]{:T(128)S(6)} %select_n.114), kind=kLoop, calls=%fused_computation.22 | loop fusion | bytes 16388 | tf_op jit(solution)/shard_map/dynamic_slice | solution.py:249
  33.4 0.3 collective-permute-done.13.refs_1_
  33.7 0.9 %shard_map.64 = f32[128,512]{1,0:T(8,128)} custom-call(bf16[128,128]{1,0:T(8,128)(2,1)S(1)} %get-tuple-element.40.heads, bf16[128,128]{1,0:T(8,128)(2,1)S(1)} %get-tuple-element.41.tails, f32[128,512]{1,0:T(8,128)S(1)} %copy-done, f32[64,512]{1,0:T(8,128)S(1)} %pad_maximum_fusion.refs_0_, f32[64,512]{1,0:T(8,128)S(1)} %collective-permute-done.13.refs_1_), custom_call_target="tpu_custom_call" | custom-call | tf_op jit(solution)/shard_map/pallas_call | solution.py:156
  (19 shorter events, 0.2 us)
Async XLA Ops:
  0.6 4.3 %copy-start.2 = (f32[16,768]{1,0:T(8,128)S(1)}, f32[16,768]{1,0:T(8,128)}, u32[]{:S(2)}) copy-start(f32[16,768]{1,0:T(8,128)} %param.4) | copy-start | bytes 147460
  0.6 9.3 %copy-start.1 = (f32[128,768]{1,0:T(8,128)S(1)}, f32[128,768]{1,0:T(8,128)}, u32[]{:S(2)}) copy-start(f32[128,768]{1,0:T(8,128)} %centers.1) | copy-start | bytes 1179652
  0.6 5.0 %collective-permute-start = (f32[16,768]{1,0:T(8,128)}, f32[16,768]{1,0:T(8,128)S(1)}, u32[]{:S(2)}, u32[]{:S(2)}) collective-permute-start(f32[16,768]{1,0:T(8,128)} %param.4), channel_id=1, source_target_pairs={{0,5},{1,16},{2,19},{3,6},{4,21},{5,0},{6,3},{7,22},{8,25},{9,12},... | collective-permute-start | bytes 147464 | tf_op jit(solution)/shard_map/ppermute | solution.py:20
  3.1 7.1 %collective-permute-start.3 = (f32[128,768]{1,0:T(8,128)}, f32[128,768]{1,0:T(8,128)S(1)}, u32[]{:S(2)}, u32[]{:S(2)}) collective-permute-start(f32[128,768]{1,0:T(8,128)} %centers.1), channel_id=1, source_target_pairs={{0,1},{1,0},{2,3},{3,2},{4,5},{5,4},{6,7},{7,6},{8,9},{9,8},{10,11... | collective-permute-start | bytes 1179656 | tf_op jit(solution)/shard_map/ppermute | solution.py:20
  4.9 5.4 %collective-permute-start.4 = (f32[128,512]{1,0:T(8,128)}, f32[128,512]{1,0:T(8,128)S(1)}, u32[]{:S(2)}, u32[]{:S(2)}) collective-permute-start(f32[128,512]{1,0:T(8,128)} %weights.3), channel_id=1, source_target_pairs={{0,1},{1,0},{2,3},{3,2},{4,5},{5,4},{6,7},{7,6},{8,9},{9,8},{10,11... | collective-permute-start | bytes 786440 | tf_op jit(solution)/shard_map/ppermute | solution.py:20
  5.7 4.5 %collective-permute-start.5 = (f32[16,768]{1,0:T(8,128)S(1)}, f32[16,768]{1,0:T(8,128)S(1)}, u32[]{:S(2)}, u32[]{:S(2)}) collective-permute-start(f32[16,768]{1,0:T(8,128)S(1)} %pad_maximum_fusion.2), channel_id=1, source_target_pairs={{0,17},{1,8},{2,11},{3,18},{4,13},{5,20},{6,23},{7,14},{8,1},{9,24... | collective-permute-start | bytes 147464 | tf_op jit(solution)/shard_map/ppermute | solution.py:20
  8.1 4.8 %collective-permute-start.1 = (f32[16,768]{1,0:T(8,128)S(1)}, f32[16,768]{1,0:T(8,128)S(1)}, u32[]{:S(2)}, u32[]{:S(2)}) collective-permute-start(f32[16,768]{1,0:T(8,128)S(1)} %pad_maximum_fusion.2), channel_id=1, source_target_pairs={{0,9},{1,4},{2,7},{3,10},{4,1},{5,12},{6,15},{7,2},{8,13},{9,0},{1... | collective-permute-start | bytes 147464 | tf_op jit(solution)/shard_map/ppermute | solution.py:20
  9.9 6.0 %collective-permute-start.2 = (f32[16,768]{1,0:T(8,128)S(1)}, f32[16,768]{1,0:T(8,128)S(1)}, u32[]{:S(2)}, u32[]{:S(2)}) collective-permute-start(f32[16,768]{1,0:T(8,128)S(1)} %pad_maximum_fusion.2), channel_id=1, source_target_pairs={{0,24},{1,13},{2,14},{3,27},{4,8},{5,29},{6,30},{7,11},{8,4},{9,17... | collective-permute-start | bytes 147464 | tf_op jit(solution)/shard_map/ppermute | solution.py:20
  10.0 1.0 %copy-start = (f32[128,512]{1,0:T(8,128)S(1)}, f32[128,512]{1,0:T(8,128)}, u32[]{:S(2)}) copy-start(f32[128,512]{1,0:T(8,128)} %weights.3) | copy-start | bytes 786436
  12.0 4.7 %collective-permute-start.6 = (f32[32,512]{1,0:T(8,128)S(1)}, f32[32,512]{1,0:T(8,128)S(1)}, u32[]{:S(2)}, u32[]{:S(2)}) collective-permute-start(f32[32,512]{1,0:T(8,128)S(1)} %get-tuple-element.35), channel_id=1, source_target_pairs={{0,9},{1,4},{2,7},{3,10},{4,1},{5,12},{6,15},{7,2},{8,13},{9,0},{1... | collective-permute-start | bytes 196616 | tf_op jit(solution)/shard_map/ppermute | solution.py:20
  16.7 3.8 %collective-permute-start.7 = (f32[32,512]{1,0:T(8,128)S(1)}, f32[32,512]{1,0:T(8,128)S(1)}, u32[]{:S(2)}, u32[]{:S(2)}) collective-permute-start(f32[32,512]{1,0:T(8,128)S(1)} %add.94), channel_id=1, source_target_pairs={{0,3},{1,16},{2,19},{3,0},{4,21},{5,6},{6,5},{7,22},{8,25},{9,10},... | collective-permute-start | bytes 196616 | tf_op jit(solution)/shard_map/ppermute | solution.py:20
  20.5 5.4 %collective-permute-start.8 = (f32[32,512]{1,0:T(8,128)S(1)}, f32[32,512]{1,0:T(8,128)S(1)}, u32[]{:S(2)}, u32[]{:S(2)}) collective-permute-start(f32[32,512]{1,0:T(8,128)S(1)} %fusion.3), channel_id=1, source_target_pairs={{0,17},{1,2},{2,1},{3,18},{4,7},{5,20},{6,23},{7,4},{8,11},{9,24},... | collective-permute-start | bytes 196616 | tf_op jit(solution)/shard_map/ppermute | solution.py:20
  25.9 3.8 %collective-permute-start.12 = (f32[32,512]{1,0:T(8,128)S(1)}, f32[32,512]{1,0:T(8,128)S(1)}, u32[]{:S(2)}, u32[]{:S(2)}) collective-permute-start(f32[32,512]{1,0:T(8,128)S(1)} %fusion.2), channel_id=1, source_target_pairs={{0,5},{1,8},{2,11},{3,6},{4,13},{5,0},{6,3},{7,14},{8,1},{9,12},{1... | collective-permute-start | bytes 196616 | tf_op jit(solution)/shard_map/ppermute | solution.py:20
  26.7 6.0 %collective-permute-start.11 = (f32[64,128]{1,0:T(8,128)S(1)}, f32[64,128]{1,0:T(8,128)S(1)}, u32[]{:S(2)}, u32[]{:S(2)}) collective-permute-start(f32[64,128]{1,0:T(8,128)S(1)} %pad_maximum_fusion.3), channel_id=1, source_target_pairs={{0,1},{1,0},{2,3},{3,2},{4,5},{5,4},{6,7},{7,6},{8,9},{9,8},{10,11... | collective-permute-start | bytes 98312 | tf_op jit(solution)/shard_map/ppermute | solution.py:20
  26.7 5.5 %collective-permute-start.10 = (f32[32,512]{1,0:T(8,128)S(1)}, f32[32,512]{1,0:T(8,128)S(1)}, u32[]{:S(2)}, u32[]{:S(2)}) collective-permute-start(f32[32,512]{1,0:T(8,128)S(1)} %fusion.2), channel_id=1, source_target_pairs={{0,12},{1,13},{2,14},{3,15},{4,8},{5,9},{6,10},{7,11},{8,4},{9,5},... | collective-permute-start | bytes 196616 | tf_op jit(solution)/shard_map/ppermute | solution.py:20
  27.6 4.6 %collective-permute-start.9 = (f32[32,512]{1,0:T(8,128)S(1)}, f32[32,512]{1,0:T(8,128)S(1)}, u32[]{:S(2)}, u32[]{:S(2)}) collective-permute-start(f32[32,512]{1,0:T(8,128)S(1)} %fusion.2), channel_id=1, source_target_pairs={{0,9},{1,4},{2,7},{3,10},{4,1},{5,12},{6,15},{7,2},{8,13},{9,0},{1... | collective-permute-start | bytes 196616 | tf_op jit(solution)/shard_map/ppermute | solution.py:20
  32.2 1.4 %collective-permute-start.13 = (f32[64,512]{1,0:T(8,128)S(1)}, f32[64,512]{1,0:T(8,128)S(1)}, u32[]{:S(2)}, u32[]{:S(2)}) collective-permute-start(f32[64,512]{1,0:T(8,128)S(1)} %pad_maximum_fusion.refs_0_), channel_id=1, source_target_pairs={{0,1},{1,0},{2,3},{3,2},{4,5},{5,4},{6,7},{7,6},{8,9},{9,8},{10,11... | collective-permute-start | bytes 393224 | tf_op jit(solution)/shard_map/ppermute | solution.py:20

commit v2 on v1

--- a/solution.py
+++ b/solution.py
@@ -124,27 +124,35 @@
     return call(functools.partial(sum_body, scale), outs, rows, *model, *taken)
 
 
-def turned_body(near, far, swapped, heads, tails):
-    kernel = jnp.concatenate([near[...], far[...], swapped[...]], axis=0)
-    heads[...], tails[...] = parted(kernel.T, 2)
+def turned_body(near, far, swapped, *outs):
+    own = jnp.concatenate([near[...], far[...]], axis=0)
+    for ref, piece in zip(outs, parted(own.T, 2) + parted(swapped[...].T, 2)):
+        ref[...] = piece
 
 
 def turned_parts(near, far, swapped):
-    count = near.shape[1]
-    shape = (count, near.shape[0] + far.shape[0] + swapped.shape[0])
-    return call(turned_body, [(shape, NARROW), (shape, NARROW)], near, far, swapped)
+    shape = (near.shape[1], swapped.shape[0])
+    a, b, c, d = call(turned_body, [(shape, NARROW)] * 4, near, far, swapped)
+    return (a, b), (c, d)
+
+
+def base_body(rate, heads, tails, weights, values, out):
+    out[...] = weights[...] - rate * contract_parts([heads[...], tails[...]], parted(values[...], 2), ((1,), (0,)))
+
+
+def base_update(rate, turned, weights, values):
+    return call(functools.partial(base_body, rate), [(weights.shape, WIDE)], *turned, weights, values)[0]
 
 
 def final_body(rate, heads, tails, weights, *refs):
     values, out, staged, sems = refs[:-3], refs[-3], refs[-2], refs[-1]
-    pieces = staged.shape[0]
-    size = staged.shape[2]
+    pieces, size = staged.shape[0], staged.shape[1]
+    value = parted(jnp.concatenate([v[...] for v in values], axis=0), 2)
     copies = []
     for i in range(pieces):
-        columns = slice(i * size, (i + 1) * size)
-        value = parted(jnp.concatenate([v[:, columns] for v in values], axis=0), 2)
-        staged[i] = weights[:, columns] - rate * contract_parts([heads[...], tails[...]], value, ((1,), (0,)))
-        copies.append(pltpu.make_async_copy(staged.at[i], out.at[:, columns], sems.at[i]))
+        part = slice(i * size, (i + 1) * size)
+        staged[i] = weights[part] - rate * contract_parts([heads[part], tails[part]], value, ((1,), (0,)))
+        copies.append(pltpu.make_async_copy(staged.at[i], out.at[part], sems.at[i]))
         copies[-1].start()
     for copy in copies:
         copy.wait()
@@ -152,21 +160,21 @@
 
 def final_update(rate, turned, weights, values):
     count, width = weights.shape
-    pieces = max(1, width // PIECE)
+    pieces = max(1, count // PIECE)
     return pl.pallas_call(
         functools.partial(final_body, rate),
         out_shape=jax.ShapeDtypeStruct(weights.shape, jnp.float32),
         in_specs=[pl.BlockSpec(memory_space=pltpu.VMEM)] * (3 + len(values)),
         out_specs=pl.BlockSpec(memory_space=pl.ANY),
         scratch_shapes=[
-            pltpu.VMEM((pieces, count, width // pieces), jnp.float32),
+            pltpu.VMEM((pieces, count // pieces, width), jnp.float32),
             pltpu.SemaphoreType.DMA((pieces,)),
         ],
         compiler_params=pltpu.CompilerParams(vmem_limit_bytes=LIMIT),
     )(*turned, weights, *values)
 
 
-PIECE = 128
+PIECE = 64
 
 
 def shards(batch, targets, centers, weights):
@@ -250,7 +258,8 @@
 
     rate = 32.0 / all_rows
 
-    new_weights = final_update(rate, turned, weights, (full, partner))
+    base = base_update(rate, turned[0], weights, full)
+    new_weights = final_update(rate, turned[1], base, (partner,))
     return (residual, new_weights)
 
 

time: 34.8 us -> 34.8 us (level)
    pallas_call x5 -> x6, Pallas kernels: 2.12 us -> 2.37 us  [call(): pl.pallas_call(body, out_shape=[jax.ShapeDtypeStruct(shape, dtype) for sh...]
  transfers between devices with their start and end apart: 14 -> 14, of which waited for: 6 -> 5; matrix products, arithmetic and copies ran while one was open for 5% -> 5% of each run, Pallas kernels for 6% -> 7%
where the time goes in v2:
time: 34.8 us; the launch traced here: 34.6 us
  starting transfers between devices  15.2 us (44%)
  waiting for transfers between devices  13 us (37%)
  Pallas kernels  3.28 us (9%)
  local copies, waits for them, and re-layouts  2.08 us (6%)
  between operations  0.82 us (2%)
    ppermute x14, starting transfers between devices, swap(): lax.ppermute(value, AXES, [(i, i ^ masks[odd(i)]) for i in range(total)])  15.2 us
    ppermute x14, waiting for transfers between devices, swap(): lax.ppermute(value, AXES, [(i, i ^ masks[odd(i)]) for i in range(total)])  13 us
    pallas_call x6, Pallas kernels, call(): pl.pallas_call(body, out_shape=[jax.ShapeDtypeStruct(shape, dtype) for sh...  2.37 us
    pallas_call x1, Pallas kernels, final_update(): pl.pallas_call(functools.partial(final_body, rate), out_shape=jax.ShapeDt...  0.91 us
    another operation x2, local copies, waits for them, and re-layouts, shards(): taken = jnp.where(mine, jnp.tile(targets, (seats, 1)), 0.0)  0.71 us
  transfers between devices with their start and end apart: 14, of which 5 were waited for; matrix products, arithmetic and copies ran while one was open for 5% of the time, Pallas kernels for 7%

profile of v2, /device:TPU:0, one launch (start us, length us, event | category | flops | bytes accessed | tf_op | source)
XLA Modules:
  0.0 34.6 jit_solution(1524575494356223992)
XLA Ops:
  0.6 0.0 copy-start.2
  0.6 0.0 copy-start.1
  0.6 2.5 %collective-permute-start = (f32[16,768]{1,0:T(8,128)}, f32[16,768]{1,0:T(8,128)S(1)}, u32[]{:S(2)}, u32[]{:S(2)}) collective-permute-start(f32[16,768]{1,0:T(8,128)} %param.4), channel_id=1, source_target_pairs={{0,5},{1,16},{2,19},{3,6},{4,21},{5,0},{6,3},{7,22},{8,25},{9,12},... | collective-permute-start | bytes 147464 | tf_op jit(solution)/shard_map/ppermute | solution.py:20
  3.1 1.8 %collective-permute-start.3 = (f32[128,768]{1,0:T(8,128)}, f32[128,768]{1,0:T(8,128)S(1)}, u32[]{:S(2)}, u32[]{:S(2)}) collective-permute-start(f32[128,768]{1,0:T(8,128)} %centers.1), channel_id=1, source_target_pairs={{0,1},{1,0},{2,3},{3,2},{4,5},{5,4},{6,7},{7,6},{8,9},{9,8},{10,11... | collective-permute-start | bytes 1179656 | tf_op jit(solution)/shard_map/ppermute | solution.py:20
  4.9 0.0 collective-permute-start.4
  4.9 0.0 copy-done.2
  5.0 0.7 %tile.4 = f32[2,4,512]{2,1,0:T(4,128)S(1)} broadcast(f32[4,512]{1,0:T(4,128)} %param.5), dimensions={1,2} | broadcast | bytes 24576 | tf_op jit(solution)/shard_map/tile | solution.py:222
  5.7 0.0 collective-permute-done
  5.7 2.4 %collective-permute-start.5 = (f32[16,768]{1,0:T(8,128)S(1)}, f32[16,768]{1,0:T(8,128)S(1)}, u32[]{:S(2)}, u32[]{:S(2)}) collective-permute-start(f32[16,768]{1,0:T(8,128)S(1)} %pad_maximum_fusion.2), channel_id=1, source_target_pairs={{0,17},{1,8},{2,11},{3,18},{4,13},{5,20},{6,23},{7,14},{8,1},{9,24... | collective-permute-start | bytes 147464 | tf_op jit(solution)/shard_map/ppermute | solution.py:20
  8.1 1.8 %collective-permute-start.1 = (f32[16,768]{1,0:T(8,128)S(1)}, f32[16,768]{1,0:T(8,128)S(1)}, u32[]{:S(2)}, u32[]{:S(2)}) collective-permute-start(f32[16,768]{1,0:T(8,128)S(1)} %pad_maximum_fusion.2), channel_id=1, source_target_pairs={{0,9},{1,4},{2,7},{3,10},{4,1},{5,12},{6,15},{7,2},{8,13},{9,0},{1... | collective-permute-start | bytes 147464 | tf_op jit(solution)/shard_map/ppermute | solution.py:20
  9.9 0.0 collective-permute-start.2
  9.9 0.1 broadcast_select_fusion.refs_12_
  10.0 0.0 copy-done.1
  10.0 0.0 copy-start
  10.0 0.2 shard_map.59
  10.2 0.0 collective-permute-done.5
  10.2 0.1 concatenate.18.rows
  10.3 0.0 collective-permute-done.4.other_weights
  10.3 0.0 collective-permute-done.3.centers
  10.3 0.7 %copy-done = f32[128,512]{1,0:T(8,128)S(1)} copy-done((f32[128,512]{1,0:T(8,128)S(1)}, f32[128,512]{1,0:T(8,128)}, u32[]{:S(2)}) %copy-start) | copy-done | bytes 262168
  10.9 0.2 shard_map.60
  11.2 0.8 %shard_map.62 = (f32[32,512]{1,0:T(8,128)S(1)}, f32[32,128]{1,0:T(8,128)S(1)}, f32[32,128]{1,0:T(8,128)S(1)}) custom-call(f32[32,768]{1,0:T(8,128)S(1)} %concatenate.18.rows, bf16[128,768]{1,0:T(8,128)(2,1)S(1)} %get-tuple-element.24.refs_0_, bf16[128,768]{1,0:T(8,128)(2,1)S(1)} %get-tuple-element.25.refs_1_, ...), custom_call_target="tpu_custom_call" | custom-call | tf_op jit(solution)/shard_map/pallas_call | solution.py:89
  12.0 0.9 %collective-permute-start.6 = (f32[32,512]{1,0:T(8,128)S(1)}, f32[32,512]{1,0:T(8,128)S(1)}, u32[]{:S(2)}, u32[]{:S(2)}) collective-permute-start(f32[32,512]{1,0:T(8,128)S(1)} %get-tuple-element.37), channel_id=1, source_target_pairs={{0,9},{1,4},{2,7},{3,10},{4,1},{5,12},{6,15},{7,2},{8,13},{9,0},{1... | collective-permute-start | bytes 196616 | tf_op jit(solution)/shard_map/ppermute | solution.py:20
  12.9 0.0 collective-permute-done.1
  12.9 3.0 %collective-permute-done.2 = f32[16,768]{1,0:T(8,128)S(1)} collective-permute-done((f32[16,768]{1,0:T(8,128)S(1)}, f32[16,768]{1,0:T(8,128)S(1)}, u32[]{:S(2)}, u32[]{:S(2)}) %collective-permute-start.2) | collective-permute-done | bytes 49184 | tf_op jit(solution)/shard_map/ppermute | solution.py:20
  15.9 0.8 %shard_map.61 = (f32[32,512]{1,0:T(8,128)S(1)}, f32[32,128]{1,0:T(8,128)S(1)}, f32[32,128]{1,0:T(8,128)S(1)}) custom-call(f32[32,768]{1,0:T(8,128)S(1)} %pad_maximum_fusion.1.rows, bf16[128,768]{1,0:T(8,128)(2,1)S(1)} %get-tuple-element.24.refs_0_, bf16[128,768]{1,0:T(8,128)(2,1)S(1)} %get-tuple-element.25.refs_1_, ...), custom_call_target="tpu_custom_call" | custom-call | tf_op jit(solution)/shard_map/pallas_call | solution.py:89
  16.7 0.0 collective-permute-done.6
  16.7 0.5 %collective-permute-start.7 = (f32[32,512]{1,0:T(8,128)S(1)}, f32[32,512]{1,0:T(8,128)S(1)}, u32[]{:S(2)}, u32[]{:S(2)}) collective-permute-start(f32[32,512]{1,0:T(8,128)S(1)} %add.94), channel_id=1, source_target_pairs={{0,3},{1,16},{2,19},{3,0},{4,21},{5,6},{6,5},{7,22},{8,25},{9,10},... | collective-permute-start | bytes 196616 | tf_op jit(solution)/shard_map/ppermute | solution.py:20
  17.3 3.2 %collective-permute-done.7 = f32[32,512]{1,0:T(8,128)S(1)} collective-permute-done((f32[32,512]{1,0:T(8,128)S(1)}, f32[32,512]{1,0:T(8,128)S(1)}, u32[]{:S(2)}, u32[]{:S(2)}) %collective-permute-start.7) | collective-permute-done | bytes 65568 | tf_op jit(solution)/shard_map/ppermute | solution.py:20
  20.5 1.9 %collective-permute-start.8 = (f32[32,512]{1,0:T(8,128)S(1)}, f32[32,512]{1,0:T(8,128)S(1)}, u32[]{:S(2)}, u32[]{:S(2)}) collective-permute-start(f32[32,512]{1,0:T(8,128)S(1)} %fusion.3), channel_id=1, source_target_pairs={{0,17},{1,2},{2,1},{3,18},{4,7},{5,20},{6,23},{7,4},{8,11},{9,24},... | collective-permute-start | bytes 196616 | tf_op jit(solution)/shard_map/ppermute | solution.py:20
  22.4 3.4 %collective-permute-done.8 = f32[32,512]{1,0:T(8,128)S(1)} collective-permute-done((f32[32,512]{1,0:T(8,128)S(1)}, f32[32,512]{1,0:T(8,128)S(1)}, u32[]{:S(2)}, u32[]{:S(2)}) %collective-permute-start.8) | collective-permute-done | bytes 65568 | tf_op jit(solution)/shard_map/ppermute | solution.py:20
  25.9 0.8 %collective-permute-start.12 = (f32[32,512]{1,0:T(8,128)S(1)}, f32[32,512]{1,0:T(8,128)S(1)}, u32[]{:S(2)}, u32[]{:S(2)}) collective-permute-start(f32[32,512]{1,0:T(8,128)S(1)} %fusion.2), channel_id=1, source_target_pairs={{0,5},{1,8},{2,11},{3,6},{4,13},{5,0},{6,3},{7,14},{8,1},{9,12},{1... | collective-permute-start | bytes 196616 | tf_op jit(solution)/shard_map/ppermute | solution.py:20
  26.7 0.0 collective-permute-start.11
  26.7 0.9 %collective-permute-start.10 = (f32[32,512]{1,0:T(8,128)S(1)}, f32[32,512]{1,0:T(8,128)S(1)}, u32[]{:S(2)}, u32[]{:S(2)}) collective-permute-start(f32[32,512]{1,0:T(8,128)S(1)} %fusion.2), channel_id=1, source_target_pairs={{0,12},{1,13},{2,14},{3,15},{4,8},{5,9},{6,10},{7,11},{8,4},{9,5},... | collective-permute-start | bytes 196616 | tf_op jit(solution)/shard_map/ppermute | solution.py:20
  27.6 1.4 %collective-permute-start.9 = (f32[32,512]{1,0:T(8,128)S(1)}, f32[32,512]{1,0:T(8,128)S(1)}, u32[]{:S(2)}, u32[]{:S(2)}) collective-permute-start(f32[32,512]{1,0:T(8,128)S(1)} %fusion.2), channel_id=1, source_target_pairs={{0,9},{1,4},{2,7},{3,10},{4,1},{5,12},{6,15},{7,2},{8,13},{9,0},{1... | collective-permute-start | bytes 196616 | tf_op jit(solution)/shard_map/ppermute | solution.py:20
  28.9 0.7 %collective-permute-done.12 = f32[32,512]{1,0:T(8,128)S(1)} collective-permute-done((f32[32,512]{1,0:T(8,128)S(1)}, f32[32,512]{1,0:T(8,128)S(1)}, u32[]{:S(2)}, u32[]{:S(2)}) %collective-permute-start.12) | collective-permute-done | bytes 65568 | tf_op jit(solution)/shard_map/ppermute | solution.py:20
  29.7 2.5 %collective-permute-done.10 = f32[32,512]{1,0:T(8,128)S(1)} collective-permute-done((f32[32,512]{1,0:T(8,128)S(1)}, f32[32,512]{1,0:T(8,128)S(1)}, u32[]{:S(2)}, u32[]{:S(2)}) %collective-permute-start.10) | collective-permute-done | bytes 65568 | tf_op jit(solution)/shard_map/ppermute | solution.py:20
  32.2 0.0 collective-permute-done.9
  32.2 0.5 %collective-permute-start.13 = (f32[64,512]{1,0:T(8,128)S(1)}, f32[64,512]{1,0:T(8,128)S(1)}, u32[]{:S(2)}, u32[]{:S(2)}) collective-permute-start(f32[64,512]{1,0:T(8,128)S(1)} %pad_maximum_fusion.values), channel_id=1, source_target_pairs={{0,1},{1,0},{2,3},{3,2},{4,5},{5,4},{6,7},{7,6},{8,9},{9,8},{10,11... | collective-permute-start | bytes 393224 | tf_op jit(solution)/shard_map/ppermute | solution.py:20
  32.7 0.0 collective-permute-done.11.swapped
  32.7 0.1 shard_map.63
  32.8 0.2 shard_map.64.weights
  33.1 0.6 %constant_dynamic-slice_fusion = f32[4,512]{1,0:T(4,128)} fusion(f32[32,512]{1,0:T(8,128)S(1)} %fusion.1, s32[]{:T(128)S(6)} %select_n.114), kind=kLoop, calls=%fused_computation.22 | loop fusion | bytes 16388 | tf_op jit(solution)/shard_map/dynamic_slice | solution.py:257
  33.7 0.0 collective-permute-done.13.refs_0_
  33.7 0.9 %shard_map.65 = f32[128,512]{1,0:T(8,128)} custom-call(bf16[128,64]{1,0:T(8,128)(2,1)S(1)} %get-tuple-element.42.heads, bf16[128,64]{1,0:T(8,128)(2,1)S(1)} %get-tuple-element.43.tails, f32[128,512]{1,0:T(8,128)S(1)} %shard_map.64.weights, f32[64,512]{1,0:T(8,128)S(1)} %collective-permute-done.13.refs_0_), custom_call_target="tpu_custom_call" | custom-call | tf_op jit(solution)/shard_map/pallas_call | solution.py:164
  (19 shorter events, 0.2 us)
Async XLA Ops:
  0.6 4.3 %copy-start.2 = (f32[16,768]{1,0:T(8,128)S(1)}, f32[16,768]{1,0:T(8,128)}, u32[]{:S(2)}) copy-start(f32[16,768]{1,0:T(8,128)} %param.4) | copy-start | bytes 147460
  0.6 9.3 %copy-start.1 = (f32[128,768]{1,0:T(8,128)S(1)}, f32[128,768]{1,0:T(8,128)}, u32[]{:S(2)}) copy-start(f32[128,768]{1,0:T(8,128)} %centers.1) | copy-start | bytes 1179652
  0.6 5.0 %collective-permute-start = (f32[16,768]{1,0:T(8,128)}, f32[16,768]{1,0:T(8,128)S(1)}, u32[]{:S(2)}, u32[]{:S(2)}) collective-permute-start(f32[16,768]{1,0:T(8,128)} %param.4), channel_id=1, source_target_pairs={{0,5},{1,16},{2,19},{3,6},{4,21},{5,0},{6,3},{7,22},{8,25},{9,12},... | collective-permute-start | bytes 147464 | tf_op jit(solution)/shard_map/ppermute | solution.py:20
  3.1 7.1 %collective-permute-start.3 = (f32[128,768]{1,0:T(8,128)}, f32[128,768]{1,0:T(8,128)S(1)}, u32[]{:S(2)}, u32[]{:S(2)}) collective-permute-start(f32[128,768]{1,0:T(8,128)} %centers.1), channel_id=1, source_target_pairs={{0,1},{1,0},{2,3},{3,2},{4,5},{5,4},{6,7},{7,6},{8,9},{9,8},{10,11... | collective-permute-start | bytes 1179656 | tf_op jit(solution)/shard_map/ppermute | solution.py:20
  4.9 5.4 %collective-permute-start.4 = (f32[128,512]{1,0:T(8,128)}, f32[128,512]{1,0:T(8,128)S(1)}, u32[]{:S(2)}, u32[]{:S(2)}) collective-permute-start(f32[128,512]{1,0:T(8,128)} %weights.3), channel_id=1, source_target_pairs={{0,1},{1,0},{2,3},{3,2},{4,5},{5,4},{6,7},{7,6},{8,9},{9,8},{10,11... | collective-permute-start | bytes 786440 | tf_op jit(solution)/shard_map/ppermute | solution.py:20
  5.7 4.5 %collective-permute-start.5 = (f32[16,768]{1,0:T(8,128)S(1)}, f32[16,768]{1,0:T(8,128)S(1)}, u32[]{:S(2)}, u32[]{:S(2)}) collective-permute-start(f32[16,768]{1,0:T(8,128)S(1)} %pad_maximum_fusion.2), channel_id=1, source_target_pairs={{0,17},{1,8},{2,11},{3,18},{4,13},{5,20},{6,23},{7,14},{8,1},{9,24... | collective-permute-start | bytes 147464 | tf_op jit(solution)/shard_map/ppermute | solution.py:20
  8.1 4.8 %collective-permute-start.1 = (f32[16,768]{1,0:T(8,128)S(1)}, f32[16,768]{1,0:T(8,128)S(1)}, u32[]{:S(2)}, u32[]{:S(2)}) collective-permute-start(f32[16,768]{1,0:T(8,128)S(1)} %pad_maximum_fusion.2), channel_id=1, source_target_pairs={{0,9},{1,4},{2,7},{3,10},{4,1},{5,12},{6,15},{7,2},{8,13},{9,0},{1... | collective-permute-start | bytes 147464 | tf_op jit(solution)/shard_map/ppermute | solution.py:20
  9.9 6.0 %collective-permute-start.2 = (f32[16,768]{1,0:T(8,128)S(1)}, f32[16,768]{1,0:T(8,128)S(1)}, u32[]{:S(2)}, u32[]{:S(2)}) collective-permute-start(f32[16,768]{1,0:T(8,128)S(1)} %pad_maximum_fusion.2), channel_id=1, source_target_pairs={{0,24},{1,13},{2,14},{3,27},{4,8},{5,29},{6,30},{7,11},{8,4},{9,17... | collective-permute-start | bytes 147464 | tf_op jit(solution)/shard_map/ppermute | solution.py:20
  10.0 1.0 %copy-start = (f32[128,512]{1,0:T(8,128)S(1)}, f32[128,512]{1,0:T(8,128)}, u32[]{:S(2)}) copy-start(f32[128,512]{1,0:T(8,128)} %weights.3) | copy-start | bytes 786436
  12.0 4.7 %collective-permute-start.6 = (f32[32,512]{1,0:T(8,128)S(1)}, f32[32,512]{1,0:T(8,128)S(1)}, u32[]{:S(2)}, u32[]{:S(2)}) collective-permute-start(f32[32,512]{1,0:T(8,128)S(1)} %get-tuple-element.37), channel_id=1, source_target_pairs={{0,9},{1,4},{2,7},{3,10},{4,1},{5,12},{6,15},{7,2},{8,13},{9,0},{1... | collective-permute-start | bytes 196616 | tf_op jit(solution)/shard_map/ppermute | solution.py:20
  16.7 3.8 %collective-permute-start.7 = (f32[32,512]{1,0:T(8,128)S(1)}, f32[32,512]{1,0:T(8,128)S(1)}, u32[]{:S(2)}, u32[]{:S(2)}) collective-permute-start(f32[32,512]{1,0:T(8,128)S(1)} %add.94), channel_id=1, source_target_pairs={{0,3},{1,16},{2,19},{3,0},{4,21},{5,6},{6,5},{7,22},{8,25},{9,10},... | collective-permute-start | bytes 196616 | tf_op jit(solution)/shard_map/ppermute | solution.py:20
  20.5 5.4 %collective-permute-start.8 = (f32[32,512]{1,0:T(8,128)S(1)}, f32[32,512]{1,0:T(8,128)S(1)}, u32[]{:S(2)}, u32[]{:S(2)}) collective-permute-start(f32[32,512]{1,0:T(8,128)S(1)} %fusion.3), channel_id=1, source_target_pairs={{0,17},{1,2},{2,1},{3,18},{4,7},{5,20},{6,23},{7,4},{8,11},{9,24},... | collective-permute-start | bytes 196616 | tf_op jit(solution)/shard_map/ppermute | solution.py:20
  25.9 3.8 %collective-permute-start.12 = (f32[32,512]{1,0:T(8,128)S(1)}, f32[32,512]{1,0:T(8,128)S(1)}, u32[]{:S(2)}, u32[]{:S(2)}) collective-permute-start(f32[32,512]{1,0:T(8,128)S(1)} %fusion.2), channel_id=1, source_target_pairs={{0,5},{1,8},{2,11},{3,6},{4,13},{5,0},{6,3},{7,14},{8,1},{9,12},{1... | collective-permute-start | bytes 196616 | tf_op jit(solution)/shard_map/ppermute | solution.py:20
  26.7 6.0 %collective-permute-start.11 = (f32[64,128]{1,0:T(8,128)S(1)}, f32[64,128]{1,0:T(8,128)S(1)}, u32[]{:S(2)}, u32[]{:S(2)}) collective-permute-start(f32[64,128]{1,0:T(8,128)S(1)} %pad_maximum_fusion.3), channel_id=1, source_target_pairs={{0,1},{1,0},{2,3},{3,2},{4,5},{5,4},{6,7},{7,6},{8,9},{9,8},{10,11... | collective-permute-start | bytes 98312 | tf_op jit(solution)/shard_map/ppermute | solution.py:20
  26.7 5.5 %collective-permute-start.10 = (f32[32,512]{1,0:T(8,128)S(1)}, f32[32,512]{1,0:T(8,128)S(1)}, u32[]{:S(2)}, u32[]{:S(2)}) collective-permute-start(f32[32,512]{1,0:T(8,128)S(1)} %fusion.2), channel_id=1, source_target_pairs={{0,12},{1,13},{2,14},{3,15},{4,8},{5,9},{6,10},{7,11},{8,4},{9,5},... | collective-permute-start | bytes 196616 | tf_op jit(solution)/shard_map/ppermute | solution.py:20
  27.6 4.6 %collective-permute-start.9 = (f32[32,512]{1,0:T(8,128)S(1)}, f32[32,512]{1,0:T(8,128)S(1)}, u32[]{:S(2)}, u32[]{:S(2)}) collective-permute-start(f32[32,512]{1,0:T(8,128)S(1)} %fusion.2), channel_id=1, source_target_pairs={{0,9},{1,4},{2,7},{3,10},{4,1},{5,12},{6,15},{7,2},{8,13},{9,0},{1... | collective-permute-start | bytes 196616 | tf_op jit(solution)/shard_map/ppermute | solution.py:20
  32.2 1.4 %collective-permute-start.13 = (f32[64,512]{1,0:T(8,128)S(1)}, f32[64,512]{1,0:T(8,128)S(1)}, u32[]{:S(2)}, u32[]{:S(2)}) collective-permute-start(f32[64,512]{1,0:T(8,128)S(1)} %pad_maximum_fusion.values), channel_id=1, source_target_pairs={{0,1},{1,0},{2,3},{3,2},{4,5},{5,4},{6,7},{7,6},{8,9},{9,8},{10,11... | collective-permute-start | bytes 393224 | tf_op jit(solution)/shard_map/ppermute | solution.py:20
